TPU v7x, 32 devices: a whole 2x2x4 slice. The times are simulated.
32 devices in a mesh: dp: 8 (over z, x), seq: 4 (over y, core).
Axes of the slice: x: 2, y: 2, z: 4, core: 2. Of those that a mesh axis runs over, the one named last changes fastest.
Arguments:
- tokens: bfloat16 [32, 6144], P('dp', 'seq'), may hold values from -6 to 6
- expert_ids: int32 [32, 2], P('dp'), may hold values from 0 to 7, all different within a row; in each aligned block of 4 rows (0 to 3, 4 to 7, ...) at most 2 rows name the same one
- router: bfloat16 [6144, 8], P('seq'), may hold values from -0.21875 to 0.21875
- w_gate: bfloat16 [5, 6144, 16384], P(None, 'seq', 'dp'), may hold values from -0.078125 to 0.078125
- w_up: bfloat16 [5, 6144, 16384], P(None, 'seq', 'dp'), may hold values from -0.078125 to 0.078125
- w_down: bfloat16 [5, 16384, 6144], P(None, 'dp', 'seq'), may hold values from -0.046875 to 0.046875
Outputs:
- mixed: bfloat16 [32, 6144], P('dp', 'seq')
Inputs may be any that keep to these rules, and one draw needn't show every extreme that they name: `expert_ids`: each row names 2 different experts. The 4 tokens of one index of dp name any expert at most 2 times, a bound that some block reaches.
All inputs are finite; a program needn't handle non-finite values.
Results may differ from a plain program's by a relative error of at most 0.0049.
Values may be sent and summed in bfloat16 or wider, within the bound.
No kernel may reach another device: no remote copies, remote signals or barrier semaphores. Data moves between devices by JAX's collectives and lax.ppermute only.
A program may use at most 192 MiB of HBM per device.

v0:
```python
import jax
import jax.numpy as jnp
from jax import lax
from jax.sharding import PartitionSpec as P

MOST = 2


def expert_rows(routes, expert, capacity):
    member = jnp.any(routes == expert, axis=1)
    position = jnp.cumsum(member.astype(jnp.int32)) - 1
    target = jnp.where(member, position, capacity)
    count_all = routes.shape[0]
    row_token = (
        jnp.zeros((capacity,), jnp.int32)
        .at[target]
        .set(jnp.arange(count_all, dtype=jnp.int32), mode="drop")
    )
    live_count = jnp.sum(member.astype(jnp.int32))
    return (row_token, jnp.maximum(position, 0), live_count)


def body(tokens, expert_ids, router, w_gate, w_up, w_down):
    gathered = lax.all_gather(tokens, "dp", axis=0, tiled=True)
    routes = lax.all_gather(expert_ids, "dp", axis=0, tiled=True)
    capacity = MOST * lax.axis_size("dp")
    block_rows = min(128, capacity)
    window_size = w_gate.shape[0]
    buffers = []
    positions = []
    live_blocks = []
    for expert in range(window_size):
        row_token, position, live_count = expert_rows(routes, expert, capacity)
        buffers.append(gathered[row_token])
        positions.append(position)
        live_blocks.append((live_count + block_rows - 1) // block_rows)
    gate_list = []
    up_list = []
    for expert in range(window_size):
        gate_part = jnp.dot(buffers[expert], w_gate[expert], preferred_element_type=jnp.float32)
        up_part = jnp.dot(buffers[expert], w_up[expert], preferred_element_type=jnp.float32)
        gate_list.append(gate_part)
        up_list.append(up_part)
    gate_parts = jnp.stack(gate_list)
    up_parts = jnp.stack(up_list)
    logit_part = jnp.dot(gathered, router, preferred_element_type=jnp.float32)
    gate_sum, up_sum, logits = lax.psum((gate_parts, up_parts, logit_part), "seq")
    hidden = (jax.nn.silu(gate_sum) * up_sum).astype(jnp.bfloat16)
    chosen = jnp.take_along_axis(logits, routes, axis=1)
    share_first = 1.0 / (1.0 + jnp.exp(chosen[:, 1] - chosen[:, 0]))
    share_second = 1.0 / (1.0 + jnp.exp(chosen[:, 0] - chosen[:, 1]))
    partial_value = jnp.zeros((gathered.shape[0], w_down.shape[2]), jnp.float32)
    for expert in range(window_size):
        expert_out = jnp.dot(hidden[expert], w_down[expert], preferred_element_type=jnp.float32)
        weighting = jnp.where(routes[:, 0] == expert, share_first, jnp.float32(0.0))
        weighting = weighting + jnp.where(routes[:, 1] == expert, share_second, jnp.float32(0.0))
        partial_value = partial_value + weighting[:, None] * expert_out[positions[expert]]
    return lax.psum_scatter(partial_value, "dp", scatter_dimension=0, tiled=True).astype(
        jnp.bfloat16
    )


def solution(mesh):
    placed = (
        P("dp", "seq"),
        P("dp", None),
        P("seq", None),
        P(None, "seq", "dp"),
        P(None, "seq", "dp"),
        P(None, "dp", "seq"),
    )
    return jax.shard_map(
        body, mesh=mesh, in_specs=placed, out_specs=P("dp", "seq"), check_vma=False
    )
```

profile of v0, /device:TPU:0, one launch (start us, length us, event | category | flops | bytes accessed | tf_op | source)
XLA Modules:
  0.0 207.5 jit_solution(11027577087069102119)
XLA Ops:
  6.5 22.7 %all-gather = s32[8,4,2]{1,2,0:T(2,128)S(1)} all-gather(s32[1,4,2]{1,2,0:T(2,128)} %bitcast.182), channel_id=1, replica_groups=mesh['dp'=8,'seq'=4] {'dp'}, dimensions={0}, use_global_device_ids=true | all-gather | bytes 288 | tf_op jit(solution)/shard_map/all_gather | solution.py:25
  29.3 0.1 copy.46
  29.4 0.1 copy.61
  29.5 0.1 copy.59
  29.6 0.1 copy.57
  29.7 0.1 copy.63
  29.8 0.1 compare_reduce_fusion
  30.0 0.1 copy.55
  30.1 0.1 copy.54
  30.2 0.1 maximum_reduce_fusion.4
  30.3 0.7 scatter_custom_fusion
  31.0 0.1 copy.60
  31.2 0.1 maximum_reduce_fusion.1
  31.3 0.7 scatter_custom_fusion.3
  32.0 0.1 copy.58
  32.1 0.1 maximum_reduce_fusion.2
  32.3 0.7 scatter_custom_fusion.2
  33.0 0.1 copy.56
  33.1 0.1 maximum_reduce_fusion.3
  33.2 0.7 scatter_custom_fusion.1
  33.9 0.1 copy.62
  34.1 0.1 maximum_reduce_fusion
  34.2 0.7 scatter_custom_fusion.4
  34.9 30.8 %all-gather.1 = bf16[8,4,1536]{2,1,0:T(4,128)(2,1)S(1)} all-gather(bf16[1,4,1536]{2,1,0:T(4,128)(2,1)} %bitcast.176), channel_id=1, replica_groups=mesh['dp'=8,'seq'=4] {'dp'}, dimensions={0}, use_global_device_ids=true | all-gather | bytes 110592 | tf_op jit(solution)/shard_map/all_gather | solution.py:24
  65.7 0.6 gather_fusion.4
  66.3 0.6 gather_fusion.3
  66.9 0.6 gather_fusion.2
  67.5 0.6 gather_fusion.1
  68.1 0.6 gather_fusion
  68.7 3.9 %fusion.48 = f32[5,16,2048]{2,1,0:T(8,128)S(1)} fusion(bf16[16,1536]{1,0:T(8,128)(2,1)S(1)} %gather_fusion, bf16[5,1536,2048]{2,1,0:T(8,128)(2,1)} %param.9), kind=kOutput, calls=%fused_computation.62 | convolution fusion | flops 100663296 | bytes 6471680 | tf_op jit(solution)/shard_map/dot_general | solution.py:40
  72.6 4.4 %fusion.78 = f32[5,16,2048]{2,1,0:T(8,128)S(1)} fusion(bf16[16,1536]{1,0:T(8,128)(2,1)S(1)} %gather_fusion, bf16[5,1536,2048]{2,1,0:T(8,128)(2,1)} %param.10), kind=kOutput, calls=%fused_computation.72 | convolution fusion | flops 100663296 | bytes 6471680 | tf_op jit(solution)/shard_map/dot_general | solution.py:41
  77.0 4.5 %fusion.54 = f32[5,16,2048]{2,1,0:T(8,128)S(1)} fusion(f32[5,16,2048]{2,1,0:T(8,128)S(1)} %fusion.48, bf16[16,1536]{1,0:T(8,128)(2,1)S(1)} %gather_fusion.1, bf16[5,1536,2048]{2,1,0:T(8,128)(2,1)} %param.9), kind=kOutput, calls=%fused_computation.64 | convolution fusion | flops 100663296 | bytes 6471680 | tf_op jit(solution)/shard_map/dot_general | solution.py:40
  81.4 4.5 %fusion.84 = f32[5,16,2048]{2,1,0:T(8,128)S(1)} fusion(f32[5,16,2048]{2,1,0:T(8,128)S(1)} %fusion.78, bf16[16,1536]{1,0:T(8,128)(2,1)S(1)} %gather_fusion.1, bf16[5,1536,2048]{2,1,0:T(8,128)(2,1)} %param.10), kind=kOutput, calls=%fused_computation.74 | convolution fusion | flops 100663296 | bytes 6471680 | tf_op jit(solution)/shard_map/dot_general | solution.py:41
  85.9 3.7 %fusion.60 = f32[5,16,2048]{2,1,0:T(8,128)S(1)} fusion(f32[5,16,2048]{2,1,0:T(8,128)S(1)} %fusion.54, bf16[16,1536]{1,0:T(8,128)(2,1)S(1)} %gather_fusion.2, bf16[5,1536,2048]{2,1,0:T(8,128)(2,1)} %param.9), kind=kOutput, calls=%fused_computation.66 | convolution fusion | flops 100663296 | bytes 6471680 | tf_op jit(solution)/shard_map/dot_general | solution.py:40
  89.6 0.9 fusion.90
  90.6 3.7 %fusion.66 = f32[5,16,2048]{2,1,0:T(8,128)S(1)} fusion(f32[5,16,2048]{2,1,0:T(8,128)S(1)} %fusion.60, bf16[16,1536]{1,0:T(8,128)(2,1)S(1)} %gather_fusion.3, bf16[5,1536,2048]{2,1,0:T(8,128)(2,1)} %param.9), kind=kOutput, calls=%fused_computation.68 | convolution fusion | flops 100663296 | bytes 6471680 | tf_op jit(solution)/shard_map/dot_general | solution.py:40
  94.3 0.9 fusion.96
  95.2 3.7 %fusion.72 = f32[5,16,2048]{2,1,0:T(8,128)S(1)} fusion(f32[5,16,2048]{2,1,0:T(8,128)S(1)} %fusion.66, bf16[16,1536]{1,0:T(8,128)(2,1)S(1)} %gather_fusion.4, bf16[5,1536,2048]{2,1,0:T(8,128)(2,1)} %param.9), kind=kOutput, calls=%fused_computation.70 | convolution fusion | flops 100663296 | bytes 6471680 | tf_op jit(solution)/shard_map/dot_general | solution.py:40
  99.0 0.9 fusion.102
  99.9 0.9 copy-done.2
  100.9 0.1 copy.51
  101.0 0.1 reshape.260
  101.1 0.1 fusion.120
  101.2 5.7 %psum.21 = f32[32,8]{0,1:T(8,128)S(1)} all-reduce(f32[32,8]{0,1:T(8,128)S(1)} %fusion.120), channel_id=1, replica_groups=mesh['dp'=8,'seq'=4] {'seq'}, use_global_device_ids=true, to_apply=%region_0.0 | all-reduce | flops 256 | bytes 2048 | tf_op jit(solution)/shard_map/psum | solution.py:47
  106.9 0.7 gather_fusion.10
  107.6 0.1 reshape.263
  107.8 0.6 dynamic-slice
  109.1 0.1 add_divide_fusion.1
  109.2 0.3 add_reduce_fusion.4
  109.4 28.0 %all-reduce.5.cloned.1.call-done = (f32[5,16,2048]{2,1,0:T(8,128)}, f32[5,16,2048]{2,1,0:T(8,128)}) async-done(((f32[5,16,2048]{2,1,0:T(8,128)}, f32[5,16,2048]{2,1,0:T(8,128)}), (f32[5,16,2048]{2,1,0:T(8,128)}, f32[5,16,2048]{2,1,0:T(8,128)})) %all-reduce.5.cloned.1.call-update) | async-done | bytes 1310736 | tf_op jit(solution)/shard_map/psum | solution.py:47
  137.4 1.5 multiply_convert_fusion
  138.9 3.7 %fusion = f32[16,1536]{1,0:T(8,128)S(1)} fusion(bf16[5,2048,1536]{2,1,0:T(8,128)(2,1)} %param.11, bf16[5,16,2048]{2,1,0:T(8,128)(2,1)S(1)} %multiply_convert_fusion), kind=kOutput, calls=%fused_computation.16 | convolution fusion | flops 100663296 | bytes 6455296 | tf_op jit(solution)/shard_map/dot_general | solution.py:54
  142.6 3.7 %fusion.2 = f32[16,1536]{1,0:T(8,128)S(1)} fusion(bf16[5,2048,1536]{2,1,0:T(8,128)(2,1)} %param.11, bf16[5,16,2048]{2,1,0:T(8,128)(2,1)S(1)} %multiply_convert_fusion), kind=kOutput, calls=%fused_computation.18 | convolution fusion | flops 100663296 | bytes 6455296 | tf_op jit(solution)/shard_map/dot_general | solution.py:54
  146.3 3.7 %fusion.4 = f32[16,1536]{1,0:T(8,128)S(1)} fusion(bf16[5,2048,1536]{2,1,0:T(8,128)(2,1)} %param.11, bf16[5,16,2048]{2,1,0:T(8,128)(2,1)S(1)} %multiply_convert_fusion), kind=kOutput, calls=%fused_computation.20 | convolution fusion | flops 100663296 | bytes 6455296 | tf_op jit(solution)/shard_map/dot_general | solution.py:54
  150.0 3.7 %fusion.6 = f32[16,1536]{1,0:T(8,128)S(1)} fusion(bf16[5,2048,1536]{2,1,0:T(8,128)(2,1)} %param.11, bf16[5,16,2048]{2,1,0:T(8,128)(2,1)S(1)} %multiply_convert_fusion), kind=kOutput, calls=%fused_computation.22 | convolution fusion | flops 100663296 | bytes 6455296 | tf_op jit(solution)/shard_map/dot_general | solution.py:54
  153.7 3.7 %fusion.8 = f32[16,1536]{1,0:T(8,128)S(1)} fusion(bf16[5,2048,1536]{2,1,0:T(8,128)(2,1)} %param.11, bf16[5,16,2048]{2,1,0:T(8,128)(2,1)S(1)} %multiply_convert_fusion), kind=kOutput, calls=%fused_computation.24 | convolution fusion | flops 100663296 | bytes 6455296 | tf_op jit(solution)/shard_map/dot_general | solution.py:54
  157.4 0.6 gather_fusion.9
  158.1 0.6 gather_fusion.8
  158.7 0.6 gather_fusion.7
  159.3 0.6 gather_fusion.5
  160.0 0.6 gather_fusion.6
  160.6 0.1 multiply_add_fusion
  160.8 39.3 %all-reduce.6 = bf16[32,1536]{1,0:T(8,128)(2,1)S(1)} all-reduce(f32[32,1536]{1,0:T(8,128)S(1)} %multiply_add_fusion), channel_id=2, replica_groups=mesh['dp'=8,'seq'=4] {'dp'}, use_global_device_ids=true, to_apply=%region_18.19.clone | all-reduce | flops 49152 | bytes 294912
  200.0 0.6 dynamic-slice_convert_fusion
  (45 shorter events, 0.6 us)
Async XLA Ops:
  6.5 94.6 %copy-start = (bf16[1536,8]{0,1:T(8,128)(2,1)S(1)}, bf16[1536,8]{0,1:T(8,128)(2,1)}, u32[]{:S(2)}) copy-start(bf16[1536,8]{0,1:T(8,128)(2,1)} %param.8) | copy-start | bytes 73732
  6.5 130.9 %all-reduce.5.cloned.1.call-start = ((), (), s32[]{:S(2)}) async-start(), calls=%async_computation | async-start | bytes 2621440 | tf_op jit(solution)/shard_map/psum | solution.py:47
  68.7 20.9 %copy-start.1 = (bf16[5,1536,2048]{2,1,0:T(8,128)(2,1)S(1)}, bf16[5,1536,2048]{2,1,0:T(8,128)(2,1)}, u32[]{:S(2)}) copy-start(bf16[5,1536,2048]{2,1,0:T(8,128)(2,1)} %param.10) | copy-start | bytes 94371840
  81.4 26.3 %copy-start.4 = (u32[32]{0:T(128)S(1)}, u32[32]{0:T(128)}, u32[]{:S(2)}) copy-start(u32[32]{0:T(128)} %constant.79) | copy-start | bytes 388
  99.0 0.9 copy-start.3
  99.9 0.9 copy-start.2
Sparse Core Ops, SparseCore 0:
  100.9 36.4 all-reduce.4
where the time goes:
time: 208 us; the launch traced here: 207 us
  blocking collectives  98.3 us (47%)
  matrix products  49.9 us (24%)
  waiting for transfers between devices  28 us (13%)
  between operations  14.4 us (7%)
  local copies, waits for them, and re-layouts  13.9 us (7%)
  other arithmetic  3.05 us (1%)
    unnamed x1, blocking collectives  39.3 us
    all_gather x1, blocking collectives, body(): gathered = lax.all_gather(tokens, 'dp', axis=0, tiled=True)  30.8 us
    psum x1, waiting for transfers between devices, body(): lax.psum((gate_parts, up_parts, logit_part), 'seq')  28 us
    all_gather x1, blocking collectives, body(): routes = lax.all_gather(expert_ids, 'dp', axis=0, tiled=True)  22.7 us
    dot_general x5, matrix products, body(): jnp.dot(buffers[expert], w_gate[expert], preferred_element_type=jnp.float32)  19.5 us
    dot_general x5, matrix products, body(): jnp.dot(hidden[expert], w_down[expert], preferred_element_type=jnp.float32)  18.6 us
    dot_general x5, matrix products, body(): jnp.dot(buffers[expert], w_up[expert], preferred_element_type=jnp.float32)  11.6 us
    psum x1, blocking collectives, body(): lax.psum((gate_parts, up_parts, logit_part), 'seq')  5.66 us
  transfers between devices with their start and end apart: 1, of which 1 were waited for; matrix products, arithmetic and copies ran while one was open for 1% of the time, Pallas kernels for 0%

commit v1 on v0

--- a/solution.py
+++ b/solution.py
@@ -22,7 +22,12 @@
 
 def body(tokens, expert_ids, router, w_gate, w_up, w_down):
     gathered = lax.all_gather(tokens, "dp", axis=0, tiled=True)
-    routes = lax.all_gather(expert_ids, "dp", axis=0, tiled=True)
+    ring = [expert_ids]
+    for hop in range(7):
+        ring.append(lax.ppermute(ring[-1], "dp", [(dev, (dev + 1) % 8) for dev in range(8)]))
+    routes = jnp.roll(
+        jnp.concatenate(ring[::-1], axis=0), (lax.axis_index("dp") + 1) * ring[0].shape[0], axis=0
+    )
     capacity = MOST * lax.axis_size("dp")
     block_rows = min(128, capacity)
     window_size = w_gate.shape[0]

time: 208 us -> 236 us (1.13)
  waiting for transfers between devices: 28 us -> 73.9 us
  blocking collectives: 98.3 us -> 76 us
  starting transfers between devices: 0.01 us -> 3.17 us
    ppermute x0 -> x7, waiting for transfers between devices: none -> 37.5 us  [body(): lax.ppermute(ring[-1], 'dp', [(dev, (dev + 1) % 8) for dev in range(8)])]
    all_gather x1 -> x0, blocking collectives: 22.7 us -> none  [body(): routes = lax.all_gather(expert_ids, 'dp', axis=0, tiled=True)]
    psum x1, waiting for transfers between devices: 28 us -> 36.4 us  [body(): lax.psum((gate_parts, up_parts, logit_part), 'seq')]
    ppermute x0 -> x7, starting transfers between devices: none -> 3.17 us  [body(): lax.ppermute(ring[-1], 'dp', [(dev, (dev + 1) % 8) for dev in range(8)])]
  transfers between devices with their start and end apart: 1 -> 8, of which waited for: 1 -> 7; matrix products, arithmetic and copies ran while one was open for 1% -> 1% of each run, Pallas kernels for 0% -> 0%
where the time goes in v1:
time: 236 us
  blocking collectives  76 us (32%)
  waiting for transfers between devices  73.9 us (31%)
  matrix products  49.8 us (21%)
  local copies, waits for them, and re-layouts  15.6 us (7%)
  between operations  14.4 us (6%)
  starting transfers between devices  3.17 us (1%)
  other arithmetic  3.12 us (1%)
    unnamed x1, blocking collectives  39.3 us
    ppermute x7, waiting for transfers between devices, body(): lax.ppermute(ring[-1], 'dp', [(dev, (dev + 1) % 8) for dev in range(8)])  37.5 us
    psum x1, waiting for transfers between devices, body(): lax.psum((gate_parts, up_parts, logit_part), 'seq')  36.4 us
    all_gather x1, blocking collectives, body(): gathered = lax.all_gather(tokens, 'dp', axis=0, tiled=True)  31.1 us
    dot_general x5, matrix products, body(): jnp.dot(buffers[expert], w_gate[expert], preferred_element_type=jnp.float32)  19.5 us
    dot_general x5, matrix products, body(): jnp.dot(hidden[expert], w_down[expert], preferred_element_type=jnp.float32)  18.6 us
    dot_general x5, matrix products, body(): jnp.dot(buffers[expert], w_up[expert], preferred_element_type=jnp.float32)  11.6 us
    psum x1, blocking collectives, body(): lax.psum((gate_parts, up_parts, logit_part), 'seq')  5.64 us
  transfers between devices with their start and end apart: 8, of which 7 were waited for; matrix products, arithmetic and copies ran while one was open for 1% of the time, Pallas kernels for 0%

profile of v1, /device:TPU:0, one launch (start us, length us, event | category | flops | bytes accessed | tf_op | source)
XLA Modules:
  0.0 236.0 jit_solution(12595302976390409670)
XLA Ops:
  6.5 3.0 %collective-permute-start = (s32[4,2]{0,1:T(2,128)}, s32[4,2]{0,1:T(2,128)S(1)}, u32[]{:S(2)}, u32[]{:S(2)}) collective-permute-start(s32[4,2]{0,1:T(2,128)} %param.7), channel_id=1, source_target_pairs={{0,4},{4,8},{8,12},{12,16},{16,20},{20,24},{24,28},{28,0},{1,5},{5... | collective-permute-start | bytes 104 | tf_op jit(solution)/shard_map/ppermute | solution.py:27
  9.5 31.1 %all-gather = bf16[8,4,1536]{2,1,0:T(4,128)(2,1)S(1)} all-gather(bf16[1,4,1536]{2,1,0:T(4,128)(2,1)} %bitcast.173), channel_id=1, replica_groups=mesh['dp'=8,'seq'=4] {'dp'}, dimensions={0}, use_global_device_ids=true | all-gather | bytes 110592 | tf_op jit(solution)/shard_map/all_gather | solution.py:24
  40.6 0.1 fusion.120
  40.8 5.6 %psum.21 = f32[32,8]{0,1:T(8,128)S(1)} all-reduce(f32[32,8]{0,1:T(8,128)S(1)} %fusion.120), channel_id=1, replica_groups=mesh['dp'=8,'seq'=4] {'seq'}, use_global_device_ids=true, to_apply=%region_0.1 | all-reduce | flops 256 | bytes 2048 | tf_op jit(solution)/shard_map/psum | solution.py:52
  46.4 1.2 dynamic-slice
  48.3 0.2 collective-permute-start.1
  48.5 6.1 %collective-permute-done.1 = s32[4,2]{0,1:T(2,128)S(1)} collective-permute-done((s32[4,2]{0,1:T(2,128)S(1)}, s32[4,2]{0,1:T(2,128)S(1)}, u32[]{:S(2)}, u32[]{:S(2)}) %collective-permute-start.1) | collective-permute-done | bytes 64 | tf_op jit(solution)/shard_map/ppermute | solution.py:27
  54.6 6.3 %collective-permute-done.2 = s32[4,2]{0,1:T(2,128)S(1)} collective-permute-done((s32[4,2]{0,1:T(2,128)S(1)}, s32[4,2]{0,1:T(2,128)S(1)}, u32[]{:S(2)}, u32[]{:S(2)}) %collective-permute-start.2) | collective-permute-done | bytes 64 | tf_op jit(solution)/shard_map/ppermute | solution.py:27
  60.9 6.3 %collective-permute-done.3 = s32[4,2]{0,1:T(2,128)S(1)} collective-permute-done((s32[4,2]{0,1:T(2,128)S(1)}, s32[4,2]{0,1:T(2,128)S(1)}, u32[]{:S(2)}, u32[]{:S(2)}) %collective-permute-start.3) | collective-permute-done | bytes 64 | tf_op jit(solution)/shard_map/ppermute | solution.py:27
  67.2 6.3 %collective-permute-done.4 = s32[4,2]{0,1:T(2,128)S(1)} collective-permute-done((s32[4,2]{0,1:T(2,128)S(1)}, s32[4,2]{0,1:T(2,128)S(1)}, u32[]{:S(2)}, u32[]{:S(2)}) %collective-permute-start.4) | collective-permute-done | bytes 64 | tf_op jit(solution)/shard_map/ppermute | solution.py:27
  73.5 6.3 %collective-permute-done.5 = s32[4,2]{0,1:T(2,128)S(1)} collective-permute-done((s32[4,2]{0,1:T(2,128)S(1)}, s32[4,2]{0,1:T(2,128)S(1)}, u32[]{:S(2)}, u32[]{:S(2)}) %collective-permute-start.5) | collective-permute-done | bytes 64 | tf_op jit(solution)/shard_map/ppermute | solution.py:27
  79.7 6.3 %collective-permute-done.6 = s32[4,2]{0,1:T(2,128)S(1)} collective-permute-done((s32[4,2]{0,1:T(2,128)S(1)}, s32[4,2]{0,1:T(2,128)S(1)}, u32[]{:S(2)}, u32[]{:S(2)}) %collective-permute-start.6) | collective-permute-done | bytes 64 | tf_op jit(solution)/shard_map/ppermute | solution.py:27
  86.0 0.9 concatenate.6
  87.0 0.2 compare_reduce_fusion
  87.3 0.1 copy.47
  87.4 0.1 copy.41
  87.5 0.1 copy.43
  87.6 0.1 copy.45
  87.7 0.1 copy.49
  87.9 0.1 maximum_reduce_fusion.2
  88.0 0.7 scatter_custom_fusion.2
  88.9 0.1 maximum_reduce_fusion
  89.0 0.7 scatter_custom_fusion.4
  89.9 0.1 maximum_reduce_fusion.4
  90.0 0.7 scatter_custom_fusion
  90.9 0.1 maximum_reduce_fusion.3
  91.0 0.7 scatter_custom_fusion.1
  91.9 0.1 maximum_reduce_fusion.1
  92.0 0.9 scatter_custom_fusion.3
  93.1 0.1 reshape.260
  93.2 0.7 gather_fusion.10
  93.9 0.1 reshape.263
  94.0 0.6 gather_fusion.4
  94.6 0.6 gather_fusion.3
  95.2 0.6 gather_fusion.2
  95.8 0.6 gather_fusion.1
  96.4 0.6 gather_fusion
  97.0 3.9 %fusion.48 = f32[5,16,2048]{2,1,0:T(8,128)S(1)} fusion(bf16[16,1536]{1,0:T(8,128)(2,1)S(1)} %gather_fusion, bf16[5,1536,2048]{2,1,0:T(8,128)(2,1)} %param.9), kind=kOutput, calls=%fused_computation.62 | convolution fusion | flops 100663296 | bytes 6471680 | tf_op jit(solution)/shard_map/dot_general | solution.py:45
  100.9 4.3 %fusion.78 = f32[5,16,2048]{2,1,0:T(8,128)S(1)} fusion(bf16[16,1536]{1,0:T(8,128)(2,1)S(1)} %gather_fusion, bf16[5,1536,2048]{2,1,0:T(8,128)(2,1)} %param.10), kind=kOutput, calls=%fused_computation.72 | convolution fusion | flops 100663296 | bytes 6471680 | tf_op jit(solution)/shard_map/dot_general | solution.py:46
  105.2 4.5 %fusion.54 = f32[5,16,2048]{2,1,0:T(8,128)S(1)} fusion(f32[5,16,2048]{2,1,0:T(8,128)S(1)} %fusion.48, bf16[16,1536]{1,0:T(8,128)(2,1)S(1)} %gather_fusion.1, bf16[5,1536,2048]{2,1,0:T(8,128)(2,1)} %param.9), kind=kOutput, calls=%fused_computation.64 | convolution fusion | flops 100663296 | bytes 6471680 | tf_op jit(solution)/shard_map/dot_general | solution.py:45
  109.7 4.5 %fusion.84 = f32[5,16,2048]{2,1,0:T(8,128)S(1)} fusion(f32[5,16,2048]{2,1,0:T(8,128)S(1)} %fusion.78, bf16[16,1536]{1,0:T(8,128)(2,1)S(1)} %gather_fusion.1, bf16[5,1536,2048]{2,1,0:T(8,128)(2,1)} %param.10), kind=kOutput, calls=%fused_computation.74 | convolution fusion | flops 100663296 | bytes 6471680 | tf_op jit(solution)/shard_map/dot_general | solution.py:46
  114.2 3.7 %fusion.60 = f32[5,16,2048]{2,1,0:T(8,128)S(1)} fusion(f32[5,16,2048]{2,1,0:T(8,128)S(1)} %fusion.54, bf16[16,1536]{1,0:T(8,128)(2,1)S(1)} %gather_fusion.2, bf16[5,1536,2048]{2,1,0:T(8,128)(2,1)} %param.9), kind=kOutput, calls=%fused_computation.66 | convolution fusion | flops 100663296 | bytes 6471680 | tf_op jit(solution)/shard_map/dot_general | solution.py:45
  117.9 0.9 fusion.90
  118.8 3.7 %fusion.66 = f32[5,16,2048]{2,1,0:T(8,128)S(1)} fusion(f32[5,16,2048]{2,1,0:T(8,128)S(1)} %fusion.60, bf16[16,1536]{1,0:T(8,128)(2,1)S(1)} %gather_fusion.3, bf16[5,1536,2048]{2,1,0:T(8,128)(2,1)} %param.9), kind=kOutput, calls=%fused_computation.68 | convolution fusion | flops 100663296 | bytes 6471680 | tf_op jit(solution)/shard_map/dot_general | solution.py:45
  122.6 0.9 fusion.96
  123.5 3.7 %fusion.72 = f32[5,16,2048]{2,1,0:T(8,128)S(1)} fusion(f32[5,16,2048]{2,1,0:T(8,128)S(1)} %fusion.66, bf16[16,1536]{1,0:T(8,128)(2,1)S(1)} %gather_fusion.4, bf16[5,1536,2048]{2,1,0:T(8,128)(2,1)} %param.9), kind=kOutput, calls=%fused_computation.70 | convolution fusion | flops 100663296 | bytes 6471680 | tf_op jit(solution)/shard_map/dot_general | solution.py:45
  127.2 0.9 fusion.102
  128.2 0.9 copy-done.3
  129.2 0.3 add_reduce_fusion.4
  129.4 36.4 %all-reduce.5.cloned.1.call-done = (f32[5,16,2048]{2,1,0:T(8,128)}, f32[5,16,2048]{2,1,0:T(8,128)}) async-done(((f32[5,16,2048]{2,1,0:T(8,128)}, f32[5,16,2048]{2,1,0:T(8,128)}), (f32[5,16,2048]{2,1,0:T(8,128)}, f32[5,16,2048]{2,1,0:T(8,128)})) %all-reduce.5.cloned.1.call-update) | async-done | bytes 1310736 | tf_op jit(solution)/shard_map/psum | solution.py:52
  165.9 1.5 multiply_convert_fusion
  167.3 3.7 %fusion = f32[16,1536]{1,0:T(8,128)S(1)} fusion(bf16[5,2048,1536]{2,1,0:T(8,128)(2,1)} %param.11, bf16[5,16,2048]{2,1,0:T(8,128)(2,1)S(1)} %multiply_convert_fusion), kind=kOutput, calls=%fused_computation.16 | convolution fusion | flops 100663296 | bytes 6455296 | tf_op jit(solution)/shard_map/dot_general | solution.py:59
  171.1 3.7 %fusion.2 = f32[16,1536]{1,0:T(8,128)S(1)} fusion(bf16[5,2048,1536]{2,1,0:T(8,128)(2,1)} %param.11, bf16[5,16,2048]{2,1,0:T(8,128)(2,1)S(1)} %multiply_convert_fusion), kind=kOutput, calls=%fused_computation.18 | convolution fusion | flops 100663296 | bytes 6455296 | tf_op jit(solution)/shard_map/dot_general | solution.py:59
  174.8 3.7 %fusion.4 = f32[16,1536]{1,0:T(8,128)S(1)} fusion(bf16[5,2048,1536]{2,1,0:T(8,128)(2,1)} %param.11, bf16[5,16,2048]{2,1,0:T(8,128)(2,1)S(1)} %multiply_convert_fusion), kind=kOutput, calls=%fused_computation.20 | convolution fusion | flops 100663296 | bytes 6455296 | tf_op jit(solution)/shard_map/dot_general | solution.py:59
  178.5 3.7 %fusion.6 = f32[16,1536]{1,0:T(8,128)S(1)} fusion(bf16[5,2048,1536]{2,1,0:T(8,128)(2,1)} %param.11, bf16[5,16,2048]{2,1,0:T(8,128)(2,1)S(1)} %multiply_convert_fusion), kind=kOutput, calls=%fused_computation.22 | convolution fusion | flops 100663296 | bytes 6455296 | tf_op jit(solution)/shard_map/dot_general | solution.py:59
  182.2 3.7 %fusion.8 = f32[16,1536]{1,0:T(8,128)S(1)} fusion(bf16[5,2048,1536]{2,1,0:T(8,128)(2,1)} %param.11, bf16[5,16,2048]{2,1,0:T(8,128)(2,1)S(1)} %multiply_convert_fusion), kind=kOutput, calls=%fused_computation.24 | convolution fusion | flops 100663296 | bytes 6455296 | tf_op jit(solution)/shard_map/dot_general | solution.py:59
  185.9 0.6 gather_fusion.9
  186.6 0.6 gather_fusion.8
  187.2 0.6 gather_fusion.7
  187.8 0.6 gather_fusion.5
  188.5 0.6 gather_fusion.6
  189.1 0.1 multiply_add_fusion
  189.3 39.3 %all-reduce.6 = bf16[32,1536]{1,0:T(8,128)(2,1)S(1)} all-reduce(f32[32,1536]{1,0:T(8,128)S(1)} %multiply_add_fusion), channel_id=2, replica_groups=mesh['dp'=8,'seq'=4] {'dp'}, use_global_device_ids=true, to_apply=%region_18.19.clone | all-reduce | flops 49152 | bytes 294912
  228.5 0.6 dynamic-slice_convert_fusion
  (59 shorter events, 1.3 us)
Async XLA Ops:
  6.5 34.1 %copy-start = (bf16[1536,8]{0,1:T(8,128)(2,1)S(1)}, bf16[1536,8]{0,1:T(8,128)(2,1)}, u32[]{:S(2)}) copy-start(bf16[1536,8]{0,1:T(8,128)(2,1)} %param.8) | copy-start | bytes 73732
  6.5 159.3 %all-reduce.5.cloned.1.call-start = ((), (), s32[]{:S(2)}) async-start(), calls=%async_computation | async-start | bytes 2621440 | tf_op jit(solution)/shard_map/psum | solution.py:52
  6.5 41.8 %collective-permute-start = (s32[4,2]{0,1:T(2,128)}, s32[4,2]{0,1:T(2,128)S(1)}, u32[]{:S(2)}, u32[]{:S(2)}) collective-permute-start(s32[4,2]{0,1:T(2,128)} %param.7), channel_id=1, source_target_pairs={{0,4},{4,8},{8,12},{12,16},{16,20},{20,24},{24,28},{28,0},{1,5},{5... | collective-permute-start | bytes 104 | tf_op jit(solution)/shard_map/ppermute | solution.py:27
  48.3 6.3 %collective-permute-start.1 = (s32[4,2]{0,1:T(2,128)S(1)}, s32[4,2]{0,1:T(2,128)S(1)}, u32[]{:S(2)}, u32[]{:S(2)}) collective-permute-start(s32[4,2]{0,1:T(2,128)S(1)} %collective-permute-done), channel_id=1, source_target_pairs={{0,4},{4,8},{8,12},{12,16},{16,20},{20,24},{24,28},{28,0},{1,5},{5... | collective-permute-start | bytes 104 | tf_op jit(solution)/shard_map/ppermute | solution.py:27
  54.6 6.3 %collective-permute-start.2 = (s32[4,2]{0,1:T(2,128)S(1)}, s32[4,2]{0,1:T(2,128)S(1)}, u32[]{:S(2)}, u32[]{:S(2)}) collective-permute-start(s32[4,2]{0,1:T(2,128)S(1)} %collective-permute-done.1), channel_id=1, source_target_pairs={{0,4},{4,8},{8,12},{12,16},{16,20},{20,24},{24,28},{28,0},{1,5},{5... | collective-permute-start | bytes 104 | tf_op jit(solution)/shard_map/ppermute | solution.py:27
  60.9 6.3 %collective-permute-start.3 = (s32[4,2]{0,1:T(2,128)S(1)}, s32[4,2]{0,1:T(2,128)S(1)}, u32[]{:S(2)}, u32[]{:S(2)}) collective-permute-start(s32[4,2]{0,1:T(2,128)S(1)} %collective-permute-done.2), channel_id=1, source_target_pairs={{0,4},{4,8},{8,12},{12,16},{16,20},{20,24},{24,28},{28,0},{1,5},{5... | collective-permute-start | bytes 104 | tf_op jit(solution)/shard_map/ppermute | solution.py:27
  67.2 6.3 %collective-permute-start.4 = (s32[4,2]{0,1:T(2,128)S(1)}, s32[4,2]{0,1:T(2,128)S(1)}, u32[]{:S(2)}, u32[]{:S(2)}) collective-permute-start(s32[4,2]{0,1:T(2,128)S(1)} %collective-permute-done.3), channel_id=1, source_target_pairs={{0,4},{4,8},{8,12},{12,16},{16,20},{20,24},{24,28},{28,0},{1,5},{5... | collective-permute-start | bytes 104 | tf_op jit(solution)/shard_map/ppermute | solution.py:27
  73.5 6.3 %collective-permute-start.5 = (s32[4,2]{0,1:T(2,128)S(1)}, s32[4,2]{0,1:T(2,128)S(1)}, u32[]{:S(2)}, u32[]{:S(2)}) collective-permute-start(s32[4,2]{0,1:T(2,128)S(1)} %collective-permute-done.4), channel_id=1, source_target_pairs={{0,4},{4,8},{8,12},{12,16},{16,20},{20,24},{24,28},{28,0},{1,5},{5... | collective-permute-start | bytes 104 | tf_op jit(solution)/shard_map/ppermute | solution.py:27
  79.7 6.3 %collective-permute-start.6 = (s32[4,2]{0,1:T(2,128)S(1)}, s32[4,2]{0,1:T(2,128)S(1)}, u32[]{:S(2)}, u32[]{:S(2)}) collective-permute-start(s32[4,2]{0,1:T(2,128)S(1)} %collective-permute-done.5), channel_id=1, source_target_pairs={{0,4},{4,8},{8,12},{12,16},{16,20},{20,24},{24,28},{28,0},{1,5},{5... | collective-permute-start | bytes 104 | tf_op jit(solution)/shard_map/ppermute | solution.py:27
  97.0 20.9 %copy-start.2 = (bf16[5,1536,2048]{2,1,0:T(8,128)(2,1)S(1)}, bf16[5,1536,2048]{2,1,0:T(8,128)(2,1)}, u32[]{:S(2)}) copy-start(bf16[5,1536,2048]{2,1,0:T(8,128)(2,1)} %param.10) | copy-start | bytes 94371840
  118.8 110.3 %copy-start.1 = (bf16[1536,8]{0,1:T(8,128)(2,1)S(1)}, bf16[1536,8]{0,1:T(8,128)(2,1)}, u32[]{:S(2)}) copy-start(bf16[1536,8]{0,1:T(8,128)(2,1)} %param.8) | copy-start | bytes 73732
  127.2 0.9 copy-start.4
  128.2 0.9 copy-start.3
Sparse Core Ops, SparseCore 0:
  129.2 36.6 all-reduce.4
